TPU v7x, 256 devices: a whole 4x4x8 slice. The times are simulated.
256 devices in a mesh: pages: 64 (over y, z, core), expert: 4 (over x).
Axes of the slice: x: 4, y: 4, z: 8, core: 2. Of those that a mesh axis runs over, the one named last changes fastest.
Arguments:
- old_keys: bfloat16 [512, 128, 2048], P('pages', None, 'expert'), may hold values from -6 to 6
- old_values: bfloat16 [512, 128, 2048], P('pages', None, 'expert'), may hold values from -6 to 6
- keep_lists: int32 [512, 31], P('pages'), may hold values from 0 to 127, as said below
- drop_weights: int32 [512, 128], P('pages'), may hold values from 1 to 8
- request_pages: int32 [64], replicated, may hold values from 4 to 12, as said below
- page_table: int32 [64, 12], replicated, may hold values from 0 to 511, as said below
- new_table: int32 [64, 3], replicated, may hold values from 0 to 255, as said below
- queries: bfloat16 [64, 2, 2048], P(None, None, 'expert'), may hold values from -20 to 20
- new_keys: bfloat16 [64, 2048], P('pages', 'expert'), may hold values from -12 to 12
- new_values: bfloat16 [64, 2048], P('pages', 'expert'), may hold values from -6 to 6
- expert_ids: int32 [64, 2], replicated, may hold values from 0 to 7, all different within a row
- router_logits: float32 [64, 8], P('pages'), may hold values from -6 to 6
- out_weight: bfloat16 [64, 2048, 256], P('pages', 'expert'), may hold values from -0.375 to 0.375
Outputs:
- compact_keys: bfloat16 [256, 128, 2048], P('pages', None, 'expert')
- compact_values: bfloat16 [256, 128, 2048], P('pages', None, 'expert')
- mixed: bfloat16 [64, 2048], P('pages', 'expert')
Inputs may be any that keep to these rules, and one draw needn't show every extreme that they name: `request_pages`: every count is a multiple of 4; the counts sum to 512; one request has 12 pages. `page_table`: the first request_pages[r] entries of row r name that request's old pages in order and later entries are unused; every old page belongs to exactly one request; old page g lies on index g // 8 of pages; no index of pages holds more than 1 old pages whose new pages lie on one index, and some index holds that many. `new_table`: the first request_pages[r] / 4 entries of row r name distinct new slots and later entries are unused; slot s lies on index s // 4 of pages; some index has all 4 of its slots used. `keep_lists`: each row holds 31 distinct positions in increasing order.
All inputs are finite; a program needn't handle non-finite values.
Results may differ from a plain program's by a relative error of at most 0.012.
Values may be sent and summed in bfloat16 or wider, within the bound.
No kernel may reach another device: no remote copies, remote signals or barrier semaphores. Data moves between devices by JAX's collectives and lax.ppermute only.
A program may use at most 64 MiB of HBM per device.

v0:
```python
import math
import jax
import jax.numpy as jnp
from jax import lax
from jax.sharding import PartitionSpec as P

HD = 128
EXPERTS = 8
NEGATIVE = -1e30


def compact_blocks(page_cache, pick_matrix, merge_coef, merge_total):
    kept_rows = jnp.einsum(
        "skt,stc->skc", pick_matrix, page_cache, preferred_element_type=jnp.float32
    )
    merged = (
        jnp.einsum("st,stc->sc", merge_coef, page_cache, preferred_element_type=jnp.float32)
        / merge_total[:, None]
    )
    return jnp.concatenate([kept_rows, merged[:, None, :]], axis=1).astype(jnp.bfloat16)


def local_scores(key_groups, group_req, group_live, queries, bias_row):
    groups, group_len, lane_width = key_groups.shape
    requests = queries.shape[0]
    topk_slots = queries.shape[1]
    head_count = lane_width // HD
    request_ids = jnp.arange(requests, dtype=jnp.int32)
    selected = (group_req[:, None] == request_ids[None, :]) & group_live[:, None]
    group_query = jnp.einsum(
        "gr,rkc->gkc", selected.astype(jnp.bfloat16), queries, preferred_element_type=jnp.float32
    ).astype(jnp.bfloat16)
    scores = jnp.einsum(
        "gkhd,glhd->gkhl",
        group_query.reshape(groups, topk_slots, head_count, HD),
        key_groups.reshape(groups, group_len, head_count, HD),
        preferred_element_type=jnp.float32,
    )
    scores = scores * (1.0 / math.sqrt(HD)) + bias_row[None, None, None, :]
    group_peak = jnp.max(scores, axis=3)
    request_peak = jnp.max(
        jnp.where(selected[:, :, None, None], group_peak[:, None, :, :], NEGATIVE), axis=0
    )
    return (selected, scores, request_peak)


def local_sums(selected, scores, value_groups, global_peak, group_live):
    groups, group_len, lane_width = value_groups.shape
    head_count = lane_width // HD
    topk_slots = scores.shape[1]
    highest = lax.Precision.HIGHEST
    chosen = selected.astype(jnp.float32)
    group_peak = jnp.einsum("gr,rkh->gkh", chosen, global_peak, precision=highest)
    terms = (
        jnp.exp(scores - group_peak[:, :, :, None])
        * group_live.astype(jnp.float32)[:, None, None, None]
    )
    numerator = jnp.einsum(
        "gkhl,glhd->gkhd",
        terms.astype(jnp.bfloat16),
        value_groups.reshape(groups, group_len, head_count, HD),
        preferred_element_type=jnp.float32,
    )
    numerator = numerator.reshape(groups, topk_slots, lane_width)
    request_num = jnp.einsum("gr,gkc->rkc", chosen, numerator, precision=highest)
    request_den = jnp.einsum("gr,gkh->rkh", chosen, jnp.sum(terms, axis=3), precision=highest)
    return (request_num, request_den)


def shards(
    old_keys,
    old_values,
    keep_lists,
    drop_weights,
    request_pages,
    page_table,
    new_table,
    queries,
    new_keys,
    new_values,
    expert_ids,
    router_logits,
    out_weight,
):
    devices = lax.axis_size("pages")
    shard_count = lax.axis_size("expert")
    my_index = lax.axis_index("pages")
    slots, page_len, lane_width = old_keys.shape
    keep_count = keep_lists.shape[1]
    block_rows = keep_count + 1
    per_new = page_len // block_rows
    requests, max_pages = page_table.shape
    max_new = new_table.shape[1]
    new_cap = 2 * (slots // per_new)
    capacity = (2 * slots + devices - 1) // devices
    head_count = lane_width // HD
    request_ids = jnp.arange(requests, dtype=jnp.int32)
    positions = jnp.arange(page_len, dtype=jnp.int32)
    picked = keep_lists[:, :, None] == positions[None, None, :]
    pick_matrix = picked.astype(jnp.bfloat16)
    merge_coef = jnp.where(jnp.any(picked, axis=1), 0.0, drop_weights.astype(jnp.float32))
    merge_total = jnp.sum(merge_coef, axis=1)
    key_blocks = compact_blocks(old_keys, pick_matrix, merge_coef.astype(jnp.bfloat16), merge_total)
    value_blocks = compact_blocks(
        old_values, pick_matrix, merge_coef.astype(jnp.bfloat16), merge_total
    )
    slot_ids = my_index * slots + jnp.arange(slots, dtype=jnp.int32)
    logical = jnp.arange(max_pages, dtype=jnp.int32)
    in_use = logical[None, :] < request_pages[:, None]
    found_at = (page_table[None, :, :] == slot_ids[:, None, None]) & in_use[None, :, :]
    owner_req = jnp.sum(jnp.where(found_at, request_ids[None, :, None], 0), axis=(1, 2))
    page_pos = jnp.sum(jnp.where(found_at, logical[None, None, :], 0), axis=(1, 2))
    fresh_slot = new_table[owner_req, page_pos // per_new]
    target_dev = fresh_slot // new_cap
    target_row = fresh_slot % new_cap * per_new + page_pos % per_new
    slot_order = jnp.arange(slots, dtype=jnp.int32)
    earlier = (target_dev[:, None] == target_dev[None, :]) & (
        slot_order[None, :] < slot_order[:, None]
    )
    send_pos = target_dev * capacity + jnp.sum(earlier, axis=1)
    outbox = send_pos[None, :] == jnp.arange(devices * capacity, dtype=jnp.int32)[:, None]
    outbox_matrix = outbox.astype(jnp.bfloat16)
    send_rows = (jnp.sum(jnp.where(outbox, target_row[None, :] + 1, 0), axis=1) - 1).reshape(
        devices, capacity
    )

    def pack_blocks(blocks):
        packed = jnp.einsum(
            "ps,sec->pec", outbox_matrix, blocks, preferred_element_type=jnp.float32
        )
        return packed.astype(jnp.bfloat16).reshape(devices, capacity, block_rows, lane_width)

    got_keys, got_values, got_rows = (
        lax.all_to_all(pack_blocks(key_blocks), "pages", split_axis=0, concat_axis=0, tiled=True),
        lax.all_to_all(pack_blocks(value_blocks), "pages", split_axis=0, concat_axis=0, tiled=True),
        lax.all_to_all(send_rows, "pages", split_axis=0, concat_axis=0, tiled=True),
    )
    landing = (
        got_rows.reshape(-1)[None, :] == jnp.arange(new_cap * per_new, dtype=jnp.int32)[:, None]
    ).astype(jnp.bfloat16)

    def land_blocks(received):
        flat_rows = received.reshape(devices * capacity, block_rows, lane_width)
        placed = jnp.einsum("qp,pec->qec", landing, flat_rows, preferred_element_type=jnp.float32)
        return placed.astype(jnp.bfloat16).reshape(new_cap, per_new * block_rows, lane_width)

    compact_keys = land_blocks(got_keys)
    compact_values = land_blocks(got_values)
    merge_bias = math.log(page_len - keep_count)
    bias_row = jnp.where(
        jnp.arange(per_new * block_rows) % block_rows == block_rows - 1, merge_bias, 0.0
    ).astype(jnp.float32)
    home_slots = my_index * new_cap + jnp.arange(new_cap, dtype=jnp.int32)
    new_live = jnp.arange(max_new, dtype=jnp.int32)[None, :] < (request_pages // per_new)[:, None]
    held_at = (new_table[None, :, :] == home_slots[:, None, None]) & new_live[None, :, :]
    group_req = jnp.sum(jnp.where(held_at, request_ids[None, :, None], 0), axis=(1, 2))
    group_live = jnp.any(held_at, axis=(1, 2))
    my_query = lax.dynamic_index_in_dim(queries, my_index, 0, keepdims=False)
    topk_slots = my_query.shape[0]
    own_score = jnp.einsum(
        "khd,hd->kh",
        my_query.reshape(topk_slots, head_count, HD),
        new_keys.reshape(head_count, HD),
        preferred_element_type=jnp.float32,
    ) * (1.0 / math.sqrt(HD))
    selected, scores, request_peak = local_scores(
        compact_keys, group_req, group_live, queries, bias_row
    )
    is_mine = (request_ids == my_index)[:, None, None]
    request_peak = jnp.where(
        is_mine, jnp.maximum(request_peak, own_score[None, :, :]), request_peak
    )
    global_peak = lax.pmax(request_peak, "pages")
    request_num, request_den = local_sums(selected, scores, compact_values, global_peak, group_live)
    my_num, my_den = (
        lax.psum_scatter(request_num, "pages", scatter_dimension=0, tiled=True),
        lax.psum_scatter(request_den, "pages", scatter_dimension=0, tiled=True),
    )
    my_peak = lax.dynamic_index_in_dim(global_peak, my_index, 0, keepdims=False)
    own_prob = jnp.exp(own_score - my_peak)
    own_rounded = lax.optimization_barrier(own_prob.astype(jnp.bfloat16)).astype(jnp.float32)
    numerator = (
        my_num[0].reshape(topk_slots, head_count, HD)
        + own_rounded[:, :, None]
        * new_values.reshape(head_count, HD).astype(jnp.float32)[None, :, :]
    )
    denominator = my_den[0] + own_prob
    my_experts = lax.dynamic_index_in_dim(expert_ids, my_index, 0, keepdims=False)
    chosen = jnp.take(router_logits[0], my_experts)
    gate_weights = jax.nn.softmax(chosen)
    weighted = (
        (gate_weights[:, None, None] * (numerator / denominator[:, :, None]))
        .astype(jnp.bfloat16)
        .reshape(1, topk_slots, lane_width)
    )
    column_blocks = devices // EXPERTS
    my_expert = my_index // column_blocks
    weight_block = out_weight[0]
    match_mask = (expert_ids == my_expert).astype(jnp.bfloat16)
    contrib = jnp.einsum(
        "rkc,rk,co->ro",
        lax.all_gather(weighted, "pages", axis=0, tiled=True),
        match_mask,
        weight_block,
        preferred_element_type=jnp.float32,
    )
    block_cols = contrib.shape[1]
    model_width = block_cols * column_blocks
    full_rows = jnp.zeros((requests, model_width), jnp.float32)
    full_rows = lax.dynamic_update_slice(
        full_rows, contrib, (jnp.zeros((), jnp.int32), my_index % column_blocks * block_cols)
    )
    spread = full_rows.reshape(requests * shard_count, model_width // shard_count)
    mixed = lax.psum_scatter(spread, ("pages", "expert"), scatter_dimension=0, tiled=True).astype(
        jnp.bfloat16
    )
    return (compact_keys, compact_values, mixed)


def solution(mesh):
    in_specs = (
        P("pages", None, "expert"),
        P("pages", None, "expert"),
        P("pages", None),
        P("pages", None),
        P(),
        P(),
        P(),
        P(None, None, "expert"),
        P("pages", "expert"),
        P("pages", "expert"),
        P(),
        P("pages", None),
        P("pages", "expert", None),
    )
    out_specs = (P("pages", None, "expert"), P("pages", None, "expert"), P("pages", "expert"))
    return jax.shard_map(shards, mesh=mesh, in_specs=in_specs, out_specs=out_specs, check_vma=False)
```

profile of v0, /device:TPU:1, one launch (start us, length us, event | category | flops | bytes accessed | tf_op | source)
XLA Modules:
  0.0 820.6 jit_solution(7523858380768102113)
XLA Ops:
  7.2 0.8 iota_compare_fusion.4
  8.0 0.9 select_reduce_fusion.1
  9.0 1.3 gather_fusion
  10.3 0.2 convert_reduce_fusion
  10.5 0.1 select_reduce_fusion.4
  10.6 0.7 copy.104
  11.3 13.2 %all-to-all-start = ((s32[64,1,1]{2,1,0:T(1,128)}), s32[64,1,1]{2,1,0:T(1,128)S(1)}, u32[]{:S(2)}, u32[]{:S(2)}) async-start(s32[64,1,1]{2,1,0:T(1,128)} %copy.104), calls=%async_computation | async-start | bytes 65536 | tf_op jit(solution)/shard_map/all_to_all | solution.py:136
  24.5 0.8 fusion.22
  25.3 1.0 convolution_convert_fusion.1
  26.3 0.8 fusion.50
  27.1 0.2 fusion.48
  27.4 0.3 fusion.46
  27.8 0.8 convert_bitcast_fusion.1
  28.6 2.5 copy.107
  31.1 2.6 all-to-all-done
  33.7 7.8 all-to-all-start.1
  41.6 1.5 convolution_convert_fusion
  43.2 0.8 convert_bitcast_fusion
  44.0 2.5 copy.112
  46.6 46.2 %all-to-all-done.1 = bf16[64,1,32,512]{3,2,1,0:T(8,128)(2,1)S(1)} async-done(((bf16[64,1,32,512]{3,2,1,0:T(8,128)(2,1)}), bf16[64,1,32,512]{3,2,1,0:T(8,128)(2,1)S(1)}, u32[]{:S(2)}, u32[]{:S(2)}) %all-to-all-start.1) | async-done | bytes 2097184 | tf_op jit(solution)/shard_map/all_to_all | solution.py:134
  92.8 6.0 all-to-all-start.2
  98.8 0.2 all-reduce.6.cloned.1.call-start
  99.1 0.2 fusion.43
  99.3 0.2 select_reduce_fusion.3
  99.5 0.1 convolution_convert_fusion.2
  99.7 0.1 fusion.60
  99.8 0.1 copy.132
  99.9 0.2 dynamic-slice_reduce_fusion.1
  100.2 0.1 copy.133
  100.3 0.6 dynamic-slice
  100.9 0.6 gather_fusion.1
  101.6 0.6 fusion.79
  102.2 1.2 fusion.77
  103.4 1.3 broadcast_divide_fusion
  104.7 1.2 reduce
  106.0 2.3 fusion.6
  108.3 0.3 copy.109
  108.6 0.1 reshape_reshape.7
  108.7 0.5 fusion.80
  109.2 0.1 copy.120
  109.3 0.1 select_reduce_fusion.2
  109.5 153.3 %pmax.7 = f32[64,2,4]{0,2,1:T(4,128)S(1)} all-reduce(f32[64,2,4]{0,2,1:T(4,128)S(1)} %maximum_select_fusion), channel_id=1, replica_groups=mesh['pages'=64,'expert'=4] {'pages'}, use_global_device_ids=true, to_apply=%region_12.13 | all-reduce | flops 512 | bytes 4096 | tf_op jit(solution)/shard_map/pmax | solution.py:173
  262.7 0.2 dynamic-slice_reduce_fusion
  262.9 0.1 fusion.57
  263.0 4.0 fusion.9
  267.0 0.3 copy.114
  267.3 0.1 copy.121
  267.4 0.2 fusion.78
  267.6 0.1 copy.125
  267.7 0.2 fusion.54
  268.0 242.0 %all-reduce.1 = f32[64,2,4]{2,1,0:T(2,128)S(1)} all-reduce(f32[64,2,4]{2,1,0:T(2,128)S(1)} %copy.126), channel_id=3, replica_groups=mesh['pages'=64,'expert'=4] {'pages'}, use_global_device_ids=true, to_apply=%region_15.16.clone | all-reduce | flops 512 | bytes 4096
  510.1 0.1 reshape_reshape.6
  510.2 0.3 convolution_bitcast_fusion
  510.5 0.3 fusion.27
  510.9 0.9 copy.124
  511.8 0.7 fusion.76
  512.6 173.4 %all-reduce.6.cloned.1.call-done = f32[64,2,512]{2,1,0:T(2,128)} async-done(((f32[64,2,512]{2,1,0:T(2,128)}), f32[64,2,512]{2,1,0:T(2,128)}) %all-reduce.6.cloned.1.call-update) | async-done | bytes 262160
  686.0 1.4 multiply_convert_fusion
  687.4 47.0 %all_gather.3 = bf16[64,2,512]{2,1,0:T(2,128)(2,1)S(1)} all-gather(bf16[1,2,512]{2,1,0:T(2,128)(2,1)S(1)} %multiply_convert_fusion), channel_id=1, replica_groups=mesh['pages'=64,'expert'=4] {'pages'}, dimensions={0}, use_global_device_ids=true | all-gather | bytes 133120 | tf_op jit(solution)/shard_map/all_gather | solution.py:202
  734.5 0.3 fusion.81
  734.8 0.2 convolution_dynamic-update-slice_fusion
  735.0 0.2 reshape.410
  735.1 78.0 %all-reduce.7 = bf16[256,512]{1,0:T(8,128)(2,1)S(1)} all-reduce(f32[256,512]{1,0:T(8,128)S(1)} %reshape.410), channel_id=4, replica_groups=mesh['pages'=64,'expert'=4] {'pages','expert'}, use_global_device_ids=true, to_apply=%region_16.17.clone | all-reduce | flops 131072 | bytes 786432
  813.1 0.6 dynamic-slice_convert_fusion
  (60 shorter events, 0.8 us)
Async XLA Ops:
  7.2 18.1 %copy-start = (bf16[8,128,512]{2,1,0:T(8,128)(2,1)S(1)}, bf16[8,128,512]{2,1,0:T(8,128)(2,1)}, u32[]{:S(2)}) copy-start(bf16[8,128,512]{2,1,0:T(8,128)(2,1)} %param.13) | copy-start | bytes 3145732
  7.2 20.2 %copy-start.3 = (bf16[8,128,512]{2,1,0:T(8,128)(2,1)S(1)}, bf16[8,128,512]{2,1,0:T(8,128)(2,1)}, u32[]{:S(2)}) copy-start(bf16[8,128,512]{2,1,0:T(8,128)(2,1)} %param.14) | copy-start | bytes 3145732
  11.3 22.4 %all-to-all-start = ((s32[64,1,1]{2,1,0:T(1,128)}), s32[64,1,1]{2,1,0:T(1,128)S(1)}, u32[]{:S(2)}, u32[]{:S(2)}) async-start(s32[64,1,1]{2,1,0:T(1,128)} %copy.104), calls=%async_computation | async-start | bytes 65536 | tf_op jit(solution)/shard_map/all_to_all | solution.py:136
  31.1 10.5 %copy-start.8 = (s32[8,31]{1,0:T(8,128)S(1)}, s32[8,31]{1,0:T(8,128)}, u32[]{:S(2)}) copy-start(s32[8,31]{1,0:T(8,128)} %param.15) | copy-start | bytes 2980
  33.7 59.1 %all-to-all-start.1 = ((bf16[64,1,32,512]{3,2,1,0:T(8,128)(2,1)}), bf16[64,1,32,512]{3,2,1,0:T(8,128)(2,1)S(1)}, u32[]{:S(2)}, u32[]{:S(2)}) async-start(bf16[64,1,32,512]{3,2,1,0:T(8,128)(2,1)} %copy.107), calls=%async_computation.1 | async-start | bytes 4194304 | tf_op jit(solution)/shard_map/all_to_all | solution.py:134
  46.5 52.5 %copy-start.11 = (s32[64]{0:T(128)S(1)}, s32[64]{0:T(128)}, u32[]{:S(2)}) copy-start(s32[64]{0:T(128)} %param.17) | copy-start | bytes 772
  46.5 52.6 %copy-start.2 = (s32[64,3]{0,1:T(4,128)S(1)}, s32[64,3]{0,1:T(4,128)}, u32[]{:S(2)}) copy-start(s32[64,3]{0,1:T(4,128)} %param.19) | copy-start | bytes 2308
  46.5 53.0 %copy-start.7 = (bf16[64,2,512]{2,1,0:T(2,128)(2,1)S(1)}, bf16[64,2,512]{2,1,0:T(2,128)(2,1)}, u32[]{:S(2)}) copy-start(bf16[64,2,512]{2,1,0:T(2,128)(2,1)} %param.20) | copy-start | bytes 393220
  46.5 53.2 %copy-start.12 = (bf16[1,512]{1,0:T(2,128)(2,1)S(1)}, bf16[1,512]{1,0:T(2,128)(2,1)}, u32[]{:S(2)}) copy-start(bf16[1,512]{1,0:T(2,128)(2,1)} %param.21) | copy-start | bytes 3076
  46.5 53.4 %copy-start.9 = (s32[64,2]{0,1:T(2,128)S(1)}, s32[64,2]{0,1:T(2,128)}, u32[]{:S(2)}) copy-start(s32[64,2]{0,1:T(2,128)} %param.23) | copy-start | bytes 1540
  46.5 53.6 %copy-start.10 = (bf16[1,512]{1,0:T(2,128)(2,1)S(1)}, bf16[1,512]{1,0:T(2,128)(2,1)}, u32[]{:S(2)}) copy-start(bf16[1,512]{1,0:T(2,128)(2,1)} %param.22) | copy-start | bytes 3076
  46.5 53.8 %copy-start.13 = (u32[256]{0:T(256)S(1)}, u32[256]{0:T(256)}, u32[]{:S(2)}) copy-start(u32[256]{0:T(256)} %constant.168) | copy-start | bytes 3076
  46.6 54.4 %copy-start.1 = (f32[1,8]{1,0:T(1,128)S(1)}, f32[1,8]{1,0:T(1,128)}, u32[]{:S(2)}) copy-start(f32[1,8]{1,0:T(1,128)} %param.24) | copy-start | bytes 100
  92.8 170.3 %all-to-all-start.2 = ((bf16[64,1,32,512]{3,2,1,0:T(8,128)(2,1)}), bf16[64,1,32,512]{3,2,1,0:T(8,128)(2,1)}, u32[]{:S(2)}, u32[]{:S(2)}) async-start(bf16[64,1,32,512]{3,2,1,0:T(8,128)(2,1)} %copy.112), calls=%async_computation.2 | async-start | bytes 4194304 | tf_op jit(solution)/shard_map/all_to_all | solution.py:135
  98.8 587.3 %all-reduce.6.cloned.1.call-start = ((), (), s32[]{:S(2)}) async-start(), calls=%async_computation.3 | async-start | bytes 524288
  108.6 158.4 %copy-start.4 = (bf16[16,32,512]{2,1,0:T(8,128)(2,1)}, bf16[16,32,512]{2,1,0:T(8,128)(2,1)S(1)}, u32[]{:S(2)}) copy-start(bf16[16,32,512]{2,1,0:T(8,128)(2,1)S(1)} %copy.109) | copy-start | bytes 1572868
  267.3 467.5 %copy-start.5 = (bf16[16,32,512]{2,1,0:T(8,128)(2,1)}, bf16[16,32,512]{2,1,0:T(8,128)(2,1)S(1)}, u32[]{:S(2)}) copy-start(bf16[16,32,512]{2,1,0:T(8,128)(2,1)S(1)} %copy.114) | copy-start | bytes 1572868
  510.1 224.7 %copy-start.6 = (bf16[1,512,256]{2,1,0:T(8,128)(2,1)S(1)}, bf16[1,512,256]{2,1,0:T(8,128)(2,1)}, u32[]{:S(2)}) copy-start(bf16[1,512,256]{2,1,0:T(8,128)(2,1)} %param.25) | copy-start | bytes 786436
Sparse Core Ops, SparseCore 0:
  511.9 174.0 all-reduce.5
where the time goes:
time: 821 us
  blocking collectives  520 us (63%)
  waiting for transfers between devices  222 us (27%)
  starting transfers between devices  27.2 us (3%)
  between operations  14.5 us (2%)
  matrix products  13.1 us (2%)
  local copies, waits for them, and re-layouts  12 us (1%)
  other arithmetic  11.1 us (1%)
    unnamed x2, blocking collectives  320 us
    unnamed x2, waiting for transfers between devices  173 us
    pmax x1, blocking collectives, shards(): global_peak = lax.pmax(request_peak, 'pages')  153 us
    all_gather x1, blocking collectives, shards(): lax.all_gather(weighted, 'pages', axis=0, tiled=True)  47 us
    all_to_all x1, waiting for transfers between devices, shards(): lax.all_to_all(pack_blocks(key_blocks), 'pages', split_axis=0, concat_axi...  46.2 us
  transfers between devices with their start and end apart: 4, of which 3 were waited for; matrix products, arithmetic and copies ran while one was open for 3% of the time, Pallas kernels for 0%

commit v1 on v0

--- a/solution.py
+++ b/solution.py
@@ -199,7 +199,9 @@
     match_mask = (expert_ids == my_expert).astype(jnp.bfloat16)
     contrib = jnp.einsum(
         "rkc,rk,co->ro",
-        lax.all_gather(weighted, "pages", axis=0, tiled=True),
+        jnp.concatenate(
+            lax.all_to_all(jnp.stack([weighted] * lax.axis_size("pages")), "pages", 0, 0), axis=0
+        ),
         match_mask,
         weight_block,
         preferred_element_type=jnp.float32,

time: 821 us -> 791 us (0.963)
  blocking collectives: 520 us -> 468 us
  waiting for transfers between devices: 222 us -> 232 us
    all_gather x1 -> x0, blocking collectives: 47 us -> none  [shards(): lax.all_gather(weighted, 'pages', axis=0, tiled=True)]
    all_to_all x0 -> x1, waiting for transfers between devices: none -> 10.2 us  [shards(): lax.all_to_all(jnp.stack([weighted] * lax.axis_size('pages')), 'pages', 0...]
  transfers between devices with their start and end apart: 4 -> 5, of which waited for: 3 -> 4; matrix products, arithmetic and copies ran while one was open for 3% -> 4% of each run, Pallas kernels for 0% -> 0%
where the time goes in v1:
time: 791 us; the launch traced here: 790 us
  blocking collectives  468 us (59%)
  waiting for transfers between devices  232 us (29%)
  starting transfers between devices  33.6 us (4%)
  local copies, waits for them, and re-layouts  16.7 us (2%)
  between operations  14.5 us (2%)
  matrix products  14.2 us (2%)
  other arithmetic  11.1 us (1%)
    unnamed x2, blocking collectives  320 us
    unnamed x2, waiting for transfers between devices  173 us
    pmax x1, blocking collectives, shards(): global_peak = lax.pmax(request_peak, 'pages')  148 us
    all_to_all x1, waiting for transfers between devices, shards(): lax.all_to_all(pack_blocks(key_blocks), 'pages', split_axis=0, concat_axi...  46.2 us
  transfers between devices with their start and end apart: 5, of which 4 were waited for; matrix products, arithmetic and copies ran while one was open for 4% of the time, Pallas kernels for 0%

profile of v1, /device:TPU:1, one launch (start us, length us, event | category | flops | bytes accessed | tf_op | source)
XLA Modules:
  0.0 790.4 jit_solution(7876076398869709167)
XLA Ops:
  7.2 0.8 iota_compare_fusion.4
  8.0 0.9 select_reduce_fusion.1
  9.0 1.3 gather_fusion
  10.3 0.2 convert_reduce_fusion
  10.6 0.7 copy.106
  11.3 13.2 %all-to-all-start = ((s32[64,1,1]{2,1,0:T(1,128)}), s32[64,1,1]{2,1,0:T(1,128)S(1)}, u32[]{:S(2)}, u32[]{:S(2)}) async-start(s32[64,1,1]{2,1,0:T(1,128)} %copy.106), calls=%async_computation | async-start | bytes 65536 | tf_op jit(solution)/shard_map/all_to_all | solution.py:136
  24.5 0.8 fusion.22
  25.3 1.0 convolution_convert_fusion.1
  26.3 0.8 fusion.52
  27.1 0.2 fusion.50
  27.4 0.3 fusion.48
  27.8 0.8 convert_bitcast_fusion.1
  28.6 2.5 copy.109
  31.1 2.6 all-to-all-done
  33.7 7.8 all-to-all-start.1
  41.6 1.5 convolution_convert_fusion
  43.1 0.8 convert_bitcast_fusion
  44.0 2.5 copy.114
  46.6 46.2 %all-to-all-done.1 = bf16[64,1,32,512]{3,2,1,0:T(8,128)(2,1)S(1)} async-done(((bf16[64,1,32,512]{3,2,1,0:T(8,128)(2,1)}), bf16[64,1,32,512]{3,2,1,0:T(8,128)(2,1)S(1)}, u32[]{:S(2)}, u32[]{:S(2)}) %all-to-all-start.1) | async-done | bytes 2097184 | tf_op jit(solution)/shard_map/all_to_all | solution.py:134
  92.8 1.3 copy-done.3
  94.1 5.8 all-to-all-start.2
  99.9 0.2 all-reduce.6.cloned.1.call-start
  100.2 0.2 fusion.45
  100.4 0.2 select_reduce_fusion.3
  100.7 0.1 convolution_convert_fusion.2
  100.8 0.1 fusion.62
  101.0 0.2 dynamic-slice_reduce_fusion.1
  101.2 0.6 dynamic-slice
  101.9 0.6 gather_fusion.1
  102.5 0.6 fusion.82
  103.1 1.2 fusion.80
  104.4 1.3 broadcast_divide_fusion
  105.7 1.2 reduce
  106.9 3.9 fusion.6
  110.8 1.1 copy.111
  111.9 2.0 reshape_reshape.7
  113.9 1.5 fusion.83
  115.3 0.1 copy.122
  115.6 148.4 %pmax.7 = f32[64,2,4]{0,2,1:T(4,128)S(1)} all-reduce(f32[64,2,4]{0,2,1:T(4,128)S(1)} %maximum_select_fusion), channel_id=1, replica_groups=mesh['pages'=64,'expert'=4] {'pages'}, use_global_device_ids=true, to_apply=%region_12.13 | all-reduce | flops 512 | bytes 4096 | tf_op jit(solution)/shard_map/pmax | solution.py:173
  264.0 0.2 dynamic-slice_reduce_fusion
  264.2 0.1 fusion.59
  264.3 2.4 fusion.9
  266.7 0.3 copy.116
  267.0 0.1 copy.123
  267.1 0.2 fusion.81
  267.3 0.1 copy.127
  267.4 0.2 fusion.56
  267.7 242.0 %all-reduce.1 = f32[64,2,4]{2,1,0:T(2,128)S(1)} all-reduce(f32[64,2,4]{2,1,0:T(2,128)S(1)} %copy.128), channel_id=3, replica_groups=mesh['pages'=64,'expert'=4] {'pages'}, use_global_device_ids=true, to_apply=%region_15.16.clone | all-reduce | flops 512 | bytes 4096
  509.7 0.1 reshape_reshape.6
  509.8 0.3 convolution_bitcast_fusion
  510.1 0.3 fusion.29
  510.5 0.9 copy.126
  511.4 0.7 fusion.79
  512.3 173.4 %all-reduce.6.cloned.1.call-done = f32[64,2,512]{2,1,0:T(2,128)} async-done(((f32[64,2,512]{2,1,0:T(2,128)}), f32[64,2,512]{2,1,0:T(2,128)}) %all-reduce.6.cloned.1.call-update) | async-done | bytes 262160
  685.6 1.4 fusion.64
  687.0 0.7 stack.3
  687.8 6.6 all-to-all-start.3
  694.3 0.1 copy.135
  694.5 10.2 %all-to-all-done.3 = bf16[64,1,2,512]{3,2,1,0:T(2,128)(2,1)S(1)} async-done(((bf16[64,1,2,512]{3,2,1,0:T(2,128)(2,1)}), bf16[64,1,2,512]{3,2,1,0:T(2,128)(2,1)S(1)}, u32[]{:S(2)}, u32[]{:S(2)}) %all-to-all-start.3) | async-done | bytes 131104 | tf_op jit(solution)/shard_map/all_to_all | solution.py:203
  704.7 0.3 fusion.23
  705.0 0.2 convolution_dynamic-update-slice_fusion
  705.2 0.1 reshape.416
  705.4 77.6 %all-reduce.7 = bf16[256,512]{1,0:T(8,128)(2,1)S(1)} all-reduce(f32[256,512]{1,0:T(8,128)S(1)} %reshape.416), channel_id=4, replica_groups=mesh['pages'=64,'expert'=4] {'pages','expert'}, use_global_device_ids=true, to_apply=%region_16.17.clone | all-reduce | flops 131072 | bytes 786432
  782.9 0.6 dynamic-slice_convert_fusion
  (62 shorter events, 1.1 us)
Async XLA Ops:
  7.2 18.1 %copy-start = (bf16[8,128,512]{2,1,0:T(8,128)(2,1)S(1)}, bf16[8,128,512]{2,1,0:T(8,128)(2,1)}, u32[]{:S(2)}) copy-start(bf16[8,128,512]{2,1,0:T(8,128)(2,1)} %param.13) | copy-start | bytes 3145732
  7.2 20.2 %copy-start.4 = (bf16[8,128,512]{2,1,0:T(8,128)(2,1)S(1)}, bf16[8,128,512]{2,1,0:T(8,128)(2,1)}, u32[]{:S(2)}) copy-start(bf16[8,128,512]{2,1,0:T(8,128)(2,1)} %param.14) | copy-start | bytes 3145732
  11.3 22.4 %all-to-all-start = ((s32[64,1,1]{2,1,0:T(1,128)}), s32[64,1,1]{2,1,0:T(1,128)S(1)}, u32[]{:S(2)}, u32[]{:S(2)}) async-start(s32[64,1,1]{2,1,0:T(1,128)} %copy.106), calls=%async_computation | async-start | bytes 65536 | tf_op jit(solution)/shard_map/all_to_all | solution.py:136
  31.1 10.5 %copy-start.8 = (s32[8,31]{1,0:T(8,128)S(1)}, s32[8,31]{1,0:T(8,128)}, u32[]{:S(2)}) copy-start(s32[8,31]{1,0:T(8,128)} %param.15) | copy-start | bytes 2980
  33.7 59.1 %all-to-all-start.1 = ((bf16[64,1,32,512]{3,2,1,0:T(8,128)(2,1)}), bf16[64,1,32,512]{3,2,1,0:T(8,128)(2,1)S(1)}, u32[]{:S(2)}, u32[]{:S(2)}) async-start(bf16[64,1,32,512]{3,2,1,0:T(8,128)(2,1)} %copy.109), calls=%async_computation.1 | async-start | bytes 4194304 | tf_op jit(solution)/shard_map/all_to_all | solution.py:134
  46.5 53.7 %copy-start.11 = (s32[64]{0:T(128)S(1)}, s32[64]{0:T(128)}, u32[]{:S(2)}) copy-start(s32[64]{0:T(128)} %param.17) | copy-start | bytes 772
  46.5 53.7 %copy-start.2 = (s32[64,3]{0,1:T(4,128)S(1)}, s32[64,3]{0,1:T(4,128)}, u32[]{:S(2)}) copy-start(s32[64,3]{0,1:T(4,128)} %param.19) | copy-start | bytes 2308
  46.5 54.2 %copy-start.7 = (bf16[64,2,512]{2,1,0:T(2,128)(2,1)S(1)}, bf16[64,2,512]{2,1,0:T(2,128)(2,1)}, u32[]{:S(2)}) copy-start(bf16[64,2,512]{2,1,0:T(2,128)(2,1)} %param.20) | copy-start | bytes 393220
  46.5 54.3 %copy-start.12 = (bf16[1,512]{1,0:T(2,128)(2,1)S(1)}, bf16[1,512]{1,0:T(2,128)(2,1)}, u32[]{:S(2)}) copy-start(bf16[1,512]{1,0:T(2,128)(2,1)} %param.21) | copy-start | bytes 3076
  46.5 54.5 %copy-start.10 = (bf16[1,512]{1,0:T(2,128)(2,1)S(1)}, bf16[1,512]{1,0:T(2,128)(2,1)}, u32[]{:S(2)}) copy-start(bf16[1,512]{1,0:T(2,128)(2,1)} %param.22) | copy-start | bytes 3076
  46.5 54.5 %copy-start.9 = (s32[64,2]{0,1:T(2,128)S(1)}, s32[64,2]{0,1:T(2,128)}, u32[]{:S(2)}) copy-start(s32[64,2]{0,1:T(2,128)} %param.23) | copy-start | bytes 1540
  46.5 54.7 %copy-start.13 = (u32[256]{0:T(256)S(1)}, u32[256]{0:T(256)}, u32[]{:S(2)}) copy-start(u32[256]{0:T(256)} %constant.168) | copy-start | bytes 3076
  46.5 55.3 %copy-start.1 = (f32[1,8]{1,0:T(1,128)S(1)}, f32[1,8]{1,0:T(1,128)}, u32[]{:S(2)}) copy-start(f32[1,8]{1,0:T(1,128)} %param.24) | copy-start | bytes 100
  92.8 1.3 copy-start.3
  94.1 170.3 %all-to-all-start.2 = ((bf16[64,1,32,512]{3,2,1,0:T(8,128)(2,1)}), bf16[64,1,32,512]{3,2,1,0:T(8,128)(2,1)S(1)}, u32[]{:S(2)}, u32[]{:S(2)}) async-start(bf16[64,1,32,512]{3,2,1,0:T(8,128)(2,1)} %copy.114), calls=%async_computation.2 | async-start | bytes 4194304 | tf_op jit(solution)/shard_map/all_to_all | solution.py:135
  99.9 585.8 %all-reduce.6.cloned.1.call-start = ((), (), s32[]{:S(2)}) async-start(), calls=%async_computation.4 | async-start | bytes 524288
  267.0 438.0 %copy-start.5 = (bf16[16,32,512]{2,1,0:T(8,128)(2,1)}, bf16[16,32,512]{2,1,0:T(8,128)(2,1)S(1)}, u32[]{:S(2)}) copy-start(bf16[16,32,512]{2,1,0:T(8,128)(2,1)S(1)} %copy.116) | copy-start | bytes 1572868
  509.8 195.2 %copy-start.6 = (bf16[1,512,256]{2,1,0:T(8,128)(2,1)S(1)}, bf16[1,512,256]{2,1,0:T(8,128)(2,1)}, u32[]{:S(2)}) copy-start(bf16[1,512,256]{2,1,0:T(8,128)(2,1)} %param.25) | copy-start | bytes 786436
  687.8 16.9 %all-to-all-start.3 = ((bf16[64,1,2,512]{3,2,1,0:T(2,128)(2,1)}), bf16[64,1,2,512]{3,2,1,0:T(2,128)(2,1)S(1)}, u32[]{:S(2)}, u32[]{:S(2)}) async-start(bf16[64,1,2,512]{3,2,1,0:T(2,128)(2,1)} %stack.3), calls=%async_computation.3 | async-start | bytes 262144 | tf_op jit(solution)/shard_map/all_to_all | solution.py:203
Sparse Core Ops, SparseCore 0:
  511.5 174.0 all-reduce.5
